TPU v7x, 512 devices: a whole 4x4x16 slice. The times are simulated.
512 devices in a mesh: dp: 128 (over y_lo, z, x), fsdp: 4 (over y_hi, core).
Axes of the slice: x: 4, y: 4 (y_hi: 2, y_lo: 2; y = y_hi * 2 + y_lo), z: 16, core: 2. Of those that a mesh axis runs over, the one named last changes fastest.
Arguments:
- cached: bfloat16 [128, 4, 256, 1024], P('dp', 'fsdp'), may hold values from -60 to 60
- send_rows: int32 [128, 4, 128, 4], P('dp', 'fsdp'), may hold values from -1 to 255, as said below
- take_rows: int32 [128, 4, 256], P('dp', 'fsdp'), may hold values from -1 to 511, as said below
- utt_index: int32 [128, 4, 256], P('dp', 'fsdp'), may hold values from 0 to 9, never falling along the last dimension, each value on 1 to 64 neighbouring positions
- upstream: bfloat16 [128, 4, 512, 1536], P('dp', 'fsdp'), may hold values from -6 to 6
- in_proj: bfloat16 [512, 1536], P(None, 'fsdp'), may hold values from -2 to 2
- norm_gain: bfloat16 [1536], P('fsdp'), may hold values from 0.099609375 to 1.8984375
- conv_kernel: bfloat16 [31, 1536], P(None, 'fsdp'), may hold values from -1 to 1
Outputs:
- grad_proj: float32 [512, 1536], P(None, 'fsdp')
- grad_kernel: float32 [31, 1536], P(None, 'fsdp')
- grad_gain: float32 [1536], P('fsdp')
- step_loss: float32 [128, 4], P('dp', 'fsdp')
Inputs may be any that keep to these rules, and one draw needn't show every extreme that they name: `send_rows`: entry [s, g, d, j] is -1 or the cache row of sender s (same fsdp group g) sent as entry j of its slot for device d. The used entries of a slot come first; a sender's used entries for one device lie in one aligned block of 4 cache rows; a sender's entries name distinct rows. Each device receives from 64 senders of its group, and some device of each group receives 4 rows from each of them. `take_rows`: entry [d, g, r] is -1 or s * 4 + j for a used entry send_rows[s, g, d, j]; each used entry is named once. The -1 entries of a device come last, the rows from one sender stand together, and some device of each group has no -1 entry. Sender 128 - 1 fills its whole slot for every device that it serves.
All inputs are finite; a program needn't handle non-finite values.
Results may differ from a plain program's by a relative error of at most 0.003.
Values may be sent and summed in bfloat16 or wider, within the bound.
A program may use at most 64 MiB of HBM per device.

v0:
```python
import jax
import jax.numpy as jnp
from jax import lax
from jax.sharding import PartitionSpec as P


def spread_conv(source_field, kernel_taps, tap_weights):
    tap_count = kernel_taps.shape[0]
    half_width = tap_count // 2
    step_count = source_field.shape[0]
    padded = jnp.pad(source_field, ((half_width, half_width), (0, 0)))
    summed = jnp.zeros_like(source_field)
    for offset in range(tap_count):
        summed = summed + kernel_taps[offset] * (
            tap_weights[:, offset : offset + 1] * padded[offset : offset + step_count]
        )
    return summed


def build_mask(live_steps, utterances, tap_count):
    half_width = tap_count // 2
    step_count = live_steps.shape[0]
    live_pad = jnp.pad(live_steps, (half_width, half_width))
    utter_pad = jnp.pad(utterances, (half_width, half_width), constant_values=-1)
    columns = []
    for offset in range(tap_count):
        columns.append(
            live_steps
            & live_pad[offset : offset + step_count]
            & (utterances == utter_pad[offset : offset + step_count])
        )
    return jnp.stack(columns, axis=1).astype(jnp.float32)


def layer_terms(encoded, live_steps, utterances, grad_above, gain, kernel):
    tap_count = kernel.shape[0]
    half_width = tap_count // 2
    step_count = encoded.shape[0]
    tap_weights = build_mask(live_steps, utterances, tap_count)
    row_mean = jnp.mean(encoded, axis=1, keepdims=True)
    centered = encoded - row_mean
    row_var = jnp.mean(centered * centered, axis=1, keepdims=True)
    inv_std = lax.rsqrt(row_var + 1e-05)
    normalized = centered * inv_std
    gain_f32 = gain.astype(jnp.float32)
    kernel_taps = kernel.astype(jnp.float32)
    normed = normalized * gain_f32
    conv_out = spread_conv(normed, kernel_taps, tap_weights)
    gate_sig = jax.nn.sigmoid(conv_out)
    output = encoded + conv_out * gate_sig
    scale = (encoded.shape[0] * encoded.shape[1]) ** (-0.5)
    grad_out = (
        jnp.where(live_steps[:, None], grad_above.astype(jnp.float32), jnp.zeros((), jnp.float32))
        * scale
    )
    device_loss = jnp.sum(output * grad_out)
    grad_conv = grad_out * (gate_sig * (1.0 + conv_out * (1.0 - gate_sig)))
    grad_normed = spread_conv(grad_conv, kernel_taps[::-1], tap_weights)
    padded = jnp.pad(normed, ((half_width, half_width), (0, 0)))
    grad_taps = jnp.stack(
        [
            jnp.sum(
                grad_conv
                * tap_weights[:, offset : offset + 1]
                * padded[offset : offset + step_count],
                axis=0,
            )
            for offset in range(tap_count)
        ]
    )
    grad_scale = jnp.sum(grad_normed * normalized, axis=0)
    grad_hat = grad_normed * gain_f32
    grad_x = grad_out + inv_std * (
        grad_hat
        - jnp.mean(grad_hat, axis=1, keepdims=True)
        - normalized * jnp.mean(grad_hat * normalized, axis=1, keepdims=True)
    )
    return (device_loss, grad_x.astype(jnp.bfloat16), grad_taps, grad_scale)


def per_device(cached, send_rows, take_rows, utt_index, upstream, in_proj, norm_gain, conv_kernel):
    cache_rows = cached[0, 0]
    wanted = send_rows[0, 0]
    outgoing = jnp.where(
        (wanted >= 0)[:, :, None],
        cache_rows[jnp.maximum(wanted, 0)],
        jnp.zeros((), cache_rows.dtype),
    )
    proj_full, taps_full, gain_full = (
        lax.all_gather(in_proj, "fsdp", axis=1, tiled=True),
        lax.all_gather(conv_kernel, "fsdp", axis=1, tiled=True),
        lax.all_gather(norm_gain[None, :], "fsdp", axis=1, tiled=True),
    )
    take_list = take_rows[0, 0]
    is_live = take_list >= 0
    safe_index = jnp.maximum(take_list, 0)
    pair_count = take_list.shape[0]
    step_width = cache_rows.shape[1] // 2
    arrived = lax.all_to_all(outgoing, "dp", split_axis=0, concat_axis=0, tiled=True)
    flat_rows = arrived.reshape(-1, arrived.shape[2])
    work_rows = jnp.where(is_live[:, None], flat_rows[safe_index], jnp.zeros((), flat_rows.dtype))
    frames = work_rows.reshape(2 * pair_count, step_width)
    encoded = jnp.dot(frames, proj_full, preferred_element_type=jnp.float32)
    live_steps = jnp.repeat(is_live, 2)
    utterances = jnp.repeat(utt_index[0, 0], 2)
    device_loss, grad_x, grad_taps, grad_scale = layer_terms(
        encoded, live_steps, utterances, upstream[0, 0], gain_full[0], taps_full
    )
    grad_weight = lax.dot_general(
        frames, grad_x, (((0,), (0,)), ((), ())), preferred_element_type=jnp.float32
    )
    shard_cols = in_proj.shape[1]
    totals = lax.psum((grad_weight, grad_taps, grad_scale[None, :]), ("dp", "fsdp"))
    col_start = lax.axis_index("fsdp") * shard_cols
    weight_part, taps_part, scale_part = [
        lax.dynamic_slice_in_dim(summed_item, col_start, shard_cols, 1) for summed_item in totals
    ]
    return (weight_part, taps_part, scale_part[0], device_loss.reshape(1, 1))


def solution(mesh):
    placed = (
        P("dp", "fsdp", None, None),
        P("dp", "fsdp", None, None),
        P("dp", "fsdp", None),
        P("dp", "fsdp", None),
        P("dp", "fsdp", None, None),
        P(None, "fsdp"),
        P("fsdp"),
        P(None, "fsdp"),
    )
    return jax.shard_map(
        per_device,
        mesh=mesh,
        in_specs=placed,
        out_specs=(P(None, "fsdp"), P(None, "fsdp"), P("fsdp"), P("dp", "fsdp")),
        check_vma=False,
    )
```

profile of v0, /device:TPU:2, one launch (start us, length us, event | category | flops | bytes accessed | tf_op | source)
XLA Modules:
  0.0 669.0 jit_solution(1528004560381405543)
XLA Ops:
  7.2 0.7 broadcast_maximum_fusion
  7.9 0.7 compare_bitcast_fusion
  8.9 2.1 gather_fusion
  10.9 0.4 reshape.99
  11.5 1.5 broadcast_select_fusion
  13.1 20.4 %all-to-all-start = ((bf16[128,4,1024]{2,1,0:T(4,128)(2,1)}), bf16[128,4,1024]{2,1,0:T(4,128)(2,1)S(1)}, u32[]{:S(2)}, u32[]{:S(2)}) async-start(bf16[128,4,1024]{2,1,0:T(4,128)(2,1)} %broadcast_select_fusion), calls=%async_computation | async-start | bytes 2097152 | tf_op jit(solution)/shard_map/all_to_all | solution.py:99
  33.6 0.7 all-gather.4.cloned.1.call-update
  35.9 0.2 stack.220
  36.1 6.7 all-gather.1
  42.8 6.9 %all_gather.10 = bf16[31,1536]{1,0:T(8,128)(2,1)S(1)} all-gather(bf16[31,384]{1,0:T(8,128)(2,1)S(1)} %copy-done.2), channel_id=1, replica_groups=mesh['dp'=128,'fsdp'=4] {'fsdp'}, dimensions={1}, use_global_device_ids=true | all-gather | bytes 119040 | tf_op jit(solution)/shard_map/all_gather | solution.py:91
  49.7 0.2 slice_reduce_fusion.29
  49.9 0.3 slice_reduce_fusion.30
  50.3 35.1 %all-to-all-done = bf16[128,4,1024]{2,1,0:T(4,128)(2,1)S(1)} async-done(((bf16[128,4,1024]{2,1,0:T(4,128)(2,1)}), bf16[128,4,1024]{2,1,0:T(4,128)(2,1)S(1)}, u32[]{:S(2)}, u32[]{:S(2)}) %all-to-all-start) | async-done | bytes 1048608 | tf_op jit(solution)/shard_map/all_to_all | solution.py:99
  85.5 0.3 reshape.93
  85.7 1.2 gather_fusion.1
  86.9 0.2 gather.10
  87.1 2.5 fusion.109
  89.6 0.5 multiply_reduce_fusion.33
  90.1 0.5 fusion.8
  90.6 0.9 copy-done.1
  91.5 31.9 %multiply_reduce_fusion.1 = (f32[1536]{0:T(1024)S(1)}, f32[1536]{0:T(1024)S(1)}, f32[1536]{0:T(1024)S(1)}, f32[1536]{0:T(1024)S(1)}, f32[1536]{0:T(1024)S(1)}, /...) fusion(f32[512,1536]{1,0:T(8,128)S(1)} %fusion.8, ...), kind=kLoop, calls=%fused_computation.10 | loop fusion | flops 102222336 | bytes 11319808 | tf_op jit(solution)/shard_map/reduce_sum | solution.py:62
  123.4 6.8 %multiply_reduce_fusion.10 = (f32[1536]{0:T(1024)S(1)}, f32[1536]{0:T(1024)S(1)}, f32[1536]{0:T(1024)S(1)}, f32[1536]{0:T(1024)S(1)}, f32[1536]{0:T(1024)S(1)}, ...) fusion(f32[512,1536]{1,0:T(8,128)S(1)} %get-tuple-element.72, ...), kind=kLoop, calls=%fused_computation.19 | loop fusion | flops 21219840 | bytes 6365184 | tf_op jit(solution)/shard_map/reduce_sum | solution.py:62
  130.2 6.6 multiply_reduce_fusion.16
  136.8 3.1 multiply_reduce_fusion.20
  140.3 28.3 %multiply_reduce_fusion = (f32[1536]{0:T(1024)S(1)}, f32[512]{0:T(512)S(1)}, f32[512]{0:T(512)S(1)}, f32[]{:T(128)}, f32[512,1536]{1,0:T(8,128)S(1)}) fusion(f32[512,1536]{1,0:T(8,128)S(1)} %get-tuple-element.137, f32[512]{0:T(512)S(1)} %add_rsqrt_fusion, f32[512]{0:T(512)S(1)} %broadcast_multiply_fusion.2, f32[1536]{0:T(1024)S(1)} %reshape.122, ...), kind=kLoop, calls=%fused_computation.9 | loop fusion | flops 86504960 | bytes 14430724 | tf_op jit(solution)/shard_map/reduce_sum | solution.py:71
  168.6 3.6 fusion.9
  172.1 2.8 stack.252
  174.9 104.0 %psum.23 = f32[1,1536]{1,0:T(1,128)S(1)} all-reduce(f32[1,1536]{1,0:T(1,128)S(1)} %broadcast_in_dim.73), channel_id=1, replica_groups=mesh['dp'=128,'fsdp'=4] {'dp','fsdp'}, use_global_device_ids=true, to_apply=%region_38.39 | all-reduce | flops 1536 | bytes 12288 | tf_op jit(solution)/shard_map/psum | solution.py:113
  279.0 0.6 dynamic-slice_reduce_fusion
  279.6 379.1 %all-reduce.7.cloned.1.call-done = (f32[512,1536]{1,0:T(8,128)}, f32[31,1536]{1,0:T(8,128)}) async-done(((f32[512,1536]{1,0:T(8,128)}, f32[31,1536]{1,0:T(8,128)}), (f32[512,1536]{1,0:T(8,128)}, f32[31,1536]{1,0:T(8,128)})) %all-reduce.7.cloned.1.call-update) | async-done | bytes 3336208 | tf_op jit(solution)/shard_map/psum | solution.py:113
  658.7 2.1 constant_dynamic-slice_fusion.1
  660.8 1.4 constant_dynamic-slice_fusion
  (105 shorter events, 2.2 us)
Async XLA Ops:
  7.2 1.7 copy-start
  10.9 23.4 %copy-start.5 = (s32[1,1,256]{2,1,0:T(1,128)S(1)}, s32[1,1,256]{2,1,0:T(1,128)}, u32[]{:S(2)}) copy-start(s32[1,1,256]{2,1,0:T(1,128)} %param.10) | copy-start | bytes 3076
  10.9 23.7 %copy-start.3 = (s32[1,1,256]{2,1,0:T(1,128)S(1)}, s32[1,1,256]{2,1,0:T(1,128)}, u32[]{:S(2)}) copy-start(s32[1,1,256]{2,1,0:T(1,128)} %param.11) | copy-start | bytes 3076
  11.4 24.7 %copy-start.4 = (bf16[384]{0:T(512)(128)(2,1)S(1)}, bf16[384]{0:T(512)(128)(2,1)}, u32[]{:S(2)}) copy-start(bf16[384]{0:T(512)(128)(2,1)} %param.14) | copy-start | bytes 2308
  11.4 31.4 %copy-start.2 = (bf16[31,384]{1,0:T(8,128)(2,1)S(1)}, bf16[31,384]{1,0:T(8,128)(2,1)}, u32[]{:S(2)}) copy-start(bf16[31,384]{1,0:T(8,128)(2,1)} %param.15) | copy-start | bytes 71428
  13.1 72.4 %all-to-all-start = ((bf16[128,4,1024]{2,1,0:T(4,128)(2,1)}), bf16[128,4,1024]{2,1,0:T(4,128)(2,1)S(1)}, u32[]{:S(2)}, u32[]{:S(2)}) async-start(bf16[128,4,1024]{2,1,0:T(4,128)(2,1)} %broadcast_select_fusion), calls=%async_computation | async-start | bytes 2097152 | tf_op jit(solution)/shard_map/all_to_all | solution.py:99
  33.5 53.6 %all-gather.4.cloned.1.call-start = ((), (), s32[]{:S(2)}) async-start(), calls=%async_computation.1 | async-start | bytes 1966080 | tf_op jit(solution)/shard_map/all_gather | solution.py:90
  34.2 624.5 %all-reduce.7.cloned.1.call-start = ((), (), s32[]{:S(2)}) async-start(), calls=%async_computation.2 | async-start | bytes 6684672 | tf_op jit(solution)/shard_map/psum | solution.py:113
  90.1 1.4 copy-start.1
Sparse Core Ops, SparseCore 0:
  36.5 35.0 all-gather.3
  175.0 483.6 all-reduce.6
where the time goes:
time: 669 us
  waiting for transfers between devices  415 us (62%)
  blocking collectives  118 us (18%)
  other arithmetic  80.9 us (12%)
  starting transfers between devices  20.5 us (3%)
  between operations  14.8 us (2%)
  local copies, waits for them, and re-layouts  14.2 us (2%)
    psum x1, waiting for transfers between devices, per_device(): lax.psum((grad_weight, grad_taps, grad_scale[None, :]), ('dp', 'fsdp'))  379 us
    psum x1, blocking collectives, per_device(): lax.psum((grad_weight, grad_taps, grad_scale[None, :]), ('dp', 'fsdp'))  104 us
    reduce_sum x4, other arithmetic, layer_terms(): jnp.sum(grad_conv * tap_weights[:, offset:offset + 1] * padded[offset:off...  48.3 us
    all_to_all x1, waiting for transfers between devices, per_device(): lax.all_to_all(outgoing, 'dp', split_axis=0, concat_axis=0, tiled=True)  35.1 us
    reduce_sum x1, other arithmetic, layer_terms(): grad_scale = jnp.sum(grad_normed * normalized, axis=0)  28.3 us
    all_to_all x1, starting transfers between devices, per_device(): lax.all_to_all(outgoing, 'dp', split_axis=0, concat_axis=0, tiled=True)  20.4 us
  transfers between devices with their start and end apart: 3, of which 2 were waited for; matrix products, arithmetic and copies ran while one was open for 1% of the time, Pallas kernels for 0%

commit v1 on v0

--- a/solution.py
+++ b/solution.py
@@ -2,6 +2,7 @@
 import jax.numpy as jnp
 from jax import lax
 from jax.sharding import PartitionSpec as P
+from jax.lax import psum
 
 
 def spread_conv(source_field, kernel_taps, tap_weights):
@@ -110,7 +111,12 @@
         frames, grad_x, (((0,), (0,)), ((), ())), preferred_element_type=jnp.float32
     )
     shard_cols = in_proj.shape[1]
-    totals = lax.psum((grad_weight, grad_taps, grad_scale[None, :]), ("dp", "fsdp"))
+
+    def patch_match(xin, peer_axis, axis_tag):
+        work_now = psum(psum(xin, peer_axis), axis_tag)
+        return work_now
+
+    totals = patch_match((grad_weight, grad_taps, grad_scale[None, :]), "dp", "fsdp")
     col_start = lax.axis_index("fsdp") * shard_cols
     weight_part, taps_part, scale_part = [
         lax.dynamic_slice_in_dim(summed_item, col_start, shard_cols, 1) for summed_item in totals

time: 669 us -> 1670 us (2.50)
  the two profiles are of different devices: /device:TPU:2 before, /device:TPU:24 now
where the time goes in v1:
time: 1670 us
  waiting for transfers between devices  1200 us (72%)
  blocking collectives  331 us (20%)
  other arithmetic  80.9 us (5%)
  starting transfers between devices  20.8 us (1%)
    psum x2, waiting for transfers between devices, patch_match(): work_now = psum(psum(xin, peer_axis), axis_tag)  1160 us
    psum x2, blocking collectives, patch_match(): work_now = psum(psum(xin, peer_axis), axis_tag)  317 us
    reduce_sum x4, other arithmetic, layer_terms(): jnp.sum(grad_conv * tap_weights[:, offset:offset + 1] * padded[offset:off...  48.3 us
    all_to_all x1, waiting for transfers between devices, per_device(): lax.all_to_all(outgoing, 'dp', split_axis=0, concat_axis=0, tiled=True)  39.4 us
  transfers between devices with their start and end apart: 4, of which 2 were waited for; matrix products, arithmetic and copies ran while one was open for 0% of the time, Pallas kernels for 0%

profile of v1, /device:TPU:24, one launch (start us, length us, event | category | flops | bytes accessed | tf_op | source)
XLA Modules:
  0.0 1669.2 jit_solution(9673941785845726212)
XLA Ops:
  7.2 0.7 broadcast_maximum_fusion
  7.9 0.7 compare_bitcast_fusion
  8.9 2.1 gather_fusion
  10.9 0.4 reshape.99
  11.5 1.5 broadcast_select_fusion
  13.1 20.7 %all-to-all-start = ((bf16[128,4,1024]{2,1,0:T(4,128)(2,1)}), bf16[128,4,1024]{2,1,0:T(4,128)(2,1)S(1)}, u32[]{:S(2)}, u32[]{:S(2)}) async-start(bf16[128,4,1024]{2,1,0:T(4,128)(2,1)} %broadcast_select_fusion), calls=%async_computation | async-start | bytes 2097152 | tf_op jit(solution)/shard_map/all_to_all | solution.py:100
  33.8 0.7 all-gather.4.cloned.1.call-update
  36.1 0.2 stack.220
  36.3 6.7 all-gather.1
  43.0 6.9 all_gather.10
  50.0 0.2 slice_reduce_fusion.29
  50.2 0.3 slice_reduce_fusion.30
  50.5 39.4 %all-to-all-done = bf16[128,4,1024]{2,1,0:T(4,128)(2,1)S(1)} async-done(((bf16[128,4,1024]{2,1,0:T(4,128)(2,1)}), bf16[128,4,1024]{2,1,0:T(4,128)(2,1)S(1)}, u32[]{:S(2)}, u32[]{:S(2)}) %all-to-all-start) | async-done | bytes 1048608 | tf_op jit(solution)/shard_map/all_to_all | solution.py:100
  89.9 0.3 reshape.93
  90.2 1.2 gather_fusion.1
  91.6 2.5 fusion.109
  94.1 0.5 multiply_reduce_fusion.33
  94.6 0.5 fusion.8
  95.0 0.9 copy-done.1
  96.0 31.9 %multiply_reduce_fusion.1 = (f32[1536]{0:T(1024)S(1)}, f32[1536]{0:T(1024)S(1)}, f32[1536]{0:T(1024)S(1)}, f32[1536]{0:T(1024)S(1)}, f32[1536]{0:T(1024)S(1)}, /...) fusion(f32[512,1536]{1,0:T(8,128)S(1)} %fusion.8, ...), kind=kLoop, calls=%fused_computation.10 | loop fusion | flops 102222336 | bytes 11319808 | tf_op jit(solution)/shard_map/reduce_sum | solution.py:63
  127.9 6.8 multiply_reduce_fusion.10
  134.6 6.6 multiply_reduce_fusion.16
  141.3 3.1 multiply_reduce_fusion.20
  144.8 28.3 %multiply_reduce_fusion = (f32[1536]{0:T(1024)S(1)}, f32[512]{0:T(512)S(1)}, f32[512]{0:T(512)S(1)}, f32[]{:T(128)}, f32[512,1536]{1,0:T(8,128)S(1)}) fusion(f32[512,1536]{1,0:T(8,128)S(1)} %get-tuple-element.139, f32[512]{0:T(512)S(1)} %add_rsqrt_fusion, f32[512]{0:T(512)S(1)} %broadcast_multiply_fusion.2, f32[1536]{0:T(1024)S(1)} %reshape.122, ...), kind=kLoop, calls=%fused_computation.9 | loop fusion | flops 86504960 | bytes 14430724 | tf_op jit(solution)/shard_map/reduce_sum | solution.py:72
  173.0 3.6 fusion.9
  176.6 2.8 stack.252
  179.4 1161.7 %all-reduce.9.cloned.1.call-done = (f32[512,1536]{1,0:T(8,128)}, f32[31,1536]{1,0:T(8,128)}) async-done(((f32[512,1536]{1,0:T(8,128)}, f32[31,1536]{1,0:T(8,128)}), (f32[512,1536]{1,0:T(8,128)}, f32[31,1536]{1,0:T(8,128)})) %all-reduce.9.cloned.1.call-update) | async-done | bytes 3336208 | tf_op jit(solution)/shard_map/psum | solution.py:116
  1341.1 310.2 %psum.46 = f32[1,1536]{1,0:T(1,128)S(1)} all-reduce(f32[1,1536]{1,0:T(1,128)S(1)} %broadcast_in_dim.73), channel_id=1, replica_groups=mesh['dp'=128,'fsdp'=4] {'dp'}, use_global_device_ids=true, to_apply=%region_40.41 | all-reduce | flops 1536 | bytes 12288 | tf_op jit(solution)/shard_map/psum | solution.py:116
  1651.3 7.3 psum.47
  1658.6 0.6 dynamic-slice_reduce_fusion
  1659.2 2.1 constant_dynamic-slice_fusion.1
  1661.3 1.4 constant_dynamic-slice_fusion
  (109 shorter events, 2.4 us)
Async XLA Ops:
  7.2 1.7 copy-start
  10.9 23.6 %copy-start.5 = (s32[1,1,256]{2,1,0:T(1,128)S(1)}, s32[1,1,256]{2,1,0:T(1,128)}, u32[]{:S(2)}) copy-start(s32[1,1,256]{2,1,0:T(1,128)} %param.10) | copy-start | bytes 3076
  10.9 23.9 %copy-start.3 = (s32[1,1,256]{2,1,0:T(1,128)S(1)}, s32[1,1,256]{2,1,0:T(1,128)}, u32[]{:S(2)}) copy-start(s32[1,1,256]{2,1,0:T(1,128)} %param.11) | copy-start | bytes 3076
  11.4 24.9 %copy-start.4 = (bf16[384]{0:T(512)(128)(2,1)S(1)}, bf16[384]{0:T(512)(128)(2,1)}, u32[]{:S(2)}) copy-start(bf16[384]{0:T(512)(128)(2,1)} %param.14) | copy-start | bytes 2308
  11.4 31.6 %copy-start.2 = (bf16[31,384]{1,0:T(8,128)(2,1)S(1)}, bf16[31,384]{1,0:T(8,128)(2,1)}, u32[]{:S(2)}) copy-start(bf16[31,384]{1,0:T(8,128)(2,1)} %param.15) | copy-start | bytes 71428
  13.1 76.8 %all-to-all-start = ((bf16[128,4,1024]{2,1,0:T(4,128)(2,1)}), bf16[128,4,1024]{2,1,0:T(4,128)(2,1)S(1)}, u32[]{:S(2)}, u32[]{:S(2)}) async-start(bf16[128,4,1024]{2,1,0:T(4,128)(2,1)} %broadcast_select_fusion), calls=%async_computation | async-start | bytes 2097152 | tf_op jit(solution)/shard_map/all_to_all | solution.py:100
  33.7 57.8 %all-gather.4.cloned.1.call-start = ((), (), s32[]{:S(2)}) async-start(), calls=%async_computation.1 | async-start | bytes 1966080 | tf_op jit(solution)/shard_map/all_gather | solution.py:91
  34.5 1306.6 %all-reduce.9.cloned.1.call-start = ((), (), s32[]{:S(2)}) async-start(), calls=%async_computation.2 | async-start | bytes 6684672 | tf_op jit(solution)/shard_map/psum | solution.py:116
  94.6 1.4 copy-start.1
  179.4 1479.8 %all-reduce.11.cloned.1.call-start = ((), (), s32[]{:S(2)}) async-start(), calls=%async_computation.3 | async-start | bytes 6684672 | tf_op jit(solution)/shard_map/psum | solution.py:116
Sparse Core Ops, SparseCore 0:
  36.7 32.5 all-gather.3
  179.5 1161.5 all-reduce.8
  1344.4 83.6 all-reduce.10
